TPU v7x, 32 devices: a whole 2x2x4 slice. The times are simulated.
32 devices in a mesh: section: 4 (over y, core), row: 2 (over x), col: 4 (over z).
Axes of the slice: x: 2, y: 2, z: 4, core: 2. Of those that a mesh axis runs over, the one named last changes fastest.
Arguments:
- incoming: bfloat16 [4, 128, 12288], P('section', 'col', 'row'), may hold values from -6 to 6
- loss_grad: bfloat16 [128, 12288], P('col', 'row'), may hold values from -6 to 6
- out_proj_t: bfloat16 [4, 12288, 6144], P('section', 'row', 'col'), may hold values from -0.0546875 to 0.0546875
- query_proj_t: bfloat16 [4, 6144, 12288], P('section', 'col', 'row'), may hold values from -0.078125 to 0.078125
- saved_query: bfloat16 [2, 4, 128, 6144], P(None, 'section', None, 'col'), may hold values from -43 to 43
- saved_key: bfloat16 [2, 4, 128, 6144], P(None, 'section', None, 'col'), may hold values from -4 to 4
- saved_value: bfloat16 [2, 4, 128, 6144], P(None, 'section', None, 'col'), may hold values from -48 to 48
- pattern: int32 [48, 2, 3], replicated, may hold values from 0 to 1, as said below
- plan: int32 [4, 2], replicated, may hold values from 0 to 1, as said below
Outputs:
- handed_first: bfloat16 [4, 128, 12288], P('section', 'col', 'row')
- handed_second: bfloat16 [4, 128, 12288], P('section', 'col', 'row')
Inputs may be any that keep to these rules, and one draw needn't show every extreme that they name: pattern[h, i, 0] = i, and every entry of pattern[h, i, :] lies between 0 and i. plan[s, 1] = (plan[s, 0] + 1) % 2.
All inputs are finite; a program needn't handle non-finite values.
Results may differ from a plain program's by a relative error of at most 0.012.
Values may be sent and summed in bfloat16 or wider, within the bound.
No kernel may reach another device: no remote copies, remote signals or barrier semaphores. Data moves between devices by JAX's collectives and lax.ppermute only.
A program may use at most 128 MiB of HBM per device.

v0:
```python
import jax
import jax.numpy as jnp
from jax import lax
from jax.sharding import PartitionSpec as P

HD = 128
BLOCK = 64


def shifted(block, axis, distance):
    devices = range(lax.axis_size(axis))
    route = [(i - distance, i) for i in devices if i - distance in devices]
    return lax.ppermute(block, axis, route)


def token_mask(pattern_part, tokens):
    blocks = tokens // BLOCK
    member = jnp.any(
        pattern_part[:, :, :, None] == jnp.arange(blocks, dtype=jnp.int32)[None, None, None, :],
        axis=2,
    )
    member = jnp.repeat(jnp.repeat(member, BLOCK, axis=1), BLOCK, axis=2)
    positions = jnp.arange(tokens, dtype=jnp.int32)
    return member & (positions[:, None] >= positions[None, :])[None]


def attend_rows(upstream, query_rows, key_rows, value_rows, allowed):
    row_count = query_rows.shape[0]
    head_count = query_rows.shape[1] // HD
    inverse_root = HD ** (-0.5)
    q_heads = query_rows.reshape(row_count, head_count, HD)
    k_heads = key_rows.reshape(key_rows.shape[0], head_count, HD)
    v_heads = value_rows.reshape(value_rows.shape[0], head_count, HD)
    up_heads = upstream.reshape(row_count, head_count, HD)
    scores = (
        jnp.einsum("thd,uhd->htu", q_heads, k_heads, preferred_element_type=jnp.float32)
        * inverse_root
    )
    masked = jnp.where(allowed, scores, -jnp.inf)
    row_peak = jnp.max(masked, axis=-1, keepdims=True)
    exp_terms = jnp.where(allowed, jnp.exp(masked - row_peak), 0.0)
    row_total = jnp.sum(exp_terms, axis=-1, keepdims=True)
    prob_rows = exp_terms / row_total
    prob_grad = jnp.einsum("thd,uhd->htu", up_heads, v_heads, preferred_element_type=jnp.float32)
    row_delta = jnp.sum(prob_rows * prob_grad, axis=-1, keepdims=True)
    dscore = (prob_rows * (prob_grad - row_delta)).astype(jnp.bfloat16)
    dquery = (
        jnp.einsum("htu,uhd->thd", dscore, k_heads, preferred_element_type=jnp.float32)
        * inverse_root
    )
    return dquery.reshape(row_count, head_count * HD).astype(jnp.bfloat16)


def body(
    incoming,
    loss_grad,
    out_proj_t,
    query_proj_t,
    saved_query,
    saved_key,
    saved_value,
    pattern,
    plan,
):
    section_at = lax.axis_index("section")
    section_count = lax.axis_size("section")
    col_at = lax.axis_index("col")
    w_out = out_proj_t[0]
    w_query = query_proj_t[0]
    head_count = w_out.shape[1] // HD
    tokens = saved_query.shape[2]
    local_pattern = lax.dynamic_slice_in_dim(pattern, col_at * head_count, head_count, 0)
    allowed = token_mask(local_pattern, tokens)

    def section_step(gradient, turn_index):
        slot_index = lax.dynamic_index_in_dim(plan[:, turn_index], section_at, 0, keepdims=False)
        query_rows = lax.dynamic_index_in_dim(saved_query[:, 0], slot_index, 0, keepdims=False)
        key_rows = lax.dynamic_index_in_dim(saved_key[:, 0], slot_index, 0, keepdims=False)
        value_rows = lax.dynamic_index_in_dim(saved_value[:, 0], slot_index, 0, keepdims=False)
        gathered = lax.all_gather(gradient, "col", axis=0, tiled=True)
        partial_value = jnp.dot(gathered, w_out, preferred_element_type=jnp.float32)
        upstream = lax.psum(partial_value, "row").astype(jnp.bfloat16)
        dquery = attend_rows(upstream, query_rows, key_rows, value_rows, allowed)
        mixed_back = lax.psum_scatter(
            jnp.dot(dquery, w_query, preferred_element_type=jnp.float32),
            "col",
            scatter_dimension=0,
            tiled=True,
        )
        return (gradient.astype(jnp.float32) + mixed_back).astype(jnp.bfloat16)

    handed_first = section_step(incoming[0], 0)
    received = shifted(handed_first, "section", -1)
    second_input = jnp.where(section_at == section_count - 1, loss_grad, received)
    handed_second = section_step(second_input, 1)
    return (handed_first[None], handed_second[None])


def solution(mesh):
    return jax.shard_map(
        body,
        mesh=mesh,
        in_specs=(
            P("section", "col", "row"),
            P("col", "row"),
            P("section", "row", "col"),
            P("section", "col", "row"),
            P(None, "section", None, "col"),
            P(None, "section", None, "col"),
            P(None, "section", None, "col"),
            P(),
            P(),
        ),
        out_specs=(P("section", "col", "row"), P("section", "col", "row")),
        check_vma=False,
    )
```

profile of v0, /device:TPU:0, one launch (start us, length us, event | category | flops | bytes accessed | tf_op | source)
XLA Modules:
  0.0 316.1 jit_solution(6484015701918346007)
XLA Ops:
  7.2 0.7 all-gather.6.cloned.1.call-update
  8.0 0.8 fusion.34
  8.7 0.6 constant_dynamic-slice_fusion.3
  13.2 1.2 constant_dynamic-slice_fusion.2
  14.4 0.2 copy.81
  15.0 1.2 constant_dynamic-slice_fusion.1
  16.4 1.2 constant_dynamic-slice_fusion
  18.0 1.4 fusion.35
  19.4 1.2 fusion.17
  20.6 28.7 %all-gather.6.cloned.1.call-done = bf16[1,128,6144]{2,1,0:T(8,128)(2,1)} async-done(((bf16[1,32,6144]{2,1,0:T(8,128)(2,1)}), bf16[1,128,6144]{2,1,0:T(8,128)(2,1)}) %all-gather.6.cloned.1.call-update) | async-done | bytes 1572880 | tf_op jit(solution)/shard_map/all_gather | solution.py:80
  49.3 8.2 %fusion.8 = f32[128,1536]{1,0:T(8,128)S(1)} fusion(bf16[1,6144,1536]{2,1,0:T(8,128)(2,1)} %param.11, bf16[1,128,6144]{2,1,0:T(8,128)(2,1)} %all-gather.6.cloned.1.call-done), kind=kOutput, calls=%fused_computation.8 | convolution fusion | flops 2415919104 | bytes 21233664 | tf_op jit(solution)/shard_map/dot_general | solution.py:81
  57.6 21.3 %all-reduce.2 = bf16[128,1536]{1,0:T(8,128)(2,1)S(1)} all-reduce(f32[128,1536]{1,0:T(8,128)S(1)} %fusion.8), channel_id=1, replica_groups=mesh['section'=4,'row'=2,'col'=4] {'row'}, use_global_device_ids=true, to_apply=%region_3.4 | all-reduce | flops 196608 | bytes 1179648 | tf_op jit(solution)/shard_map/psum | solution.py:82
  79.1 2.4 multiply_reduce_fusion.1
  81.5 2.2 fusion.22
  83.7 0.2 copy.57
  83.9 10.8 %fusion.4 = f32[128,6144]{1,0:T(8,128)} fusion(bf16[128,1536]{0,1:T(8,128)(2,1)S(1)} %bitcast.58, bf16[1,1536,6144]{2,1,0:T(8,128)(2,1)} %param.12), kind=kOutput, calls=%fused_computation.4 | convolution fusion | flops 2415919104 | bytes 22413312 | tf_op jit(solution)/shard_map/dot_general | solution.py:85
  94.8 60.4 %reduce-scatter.3.cloned.1.call-done = f32[32,6144]{1,0:T(8,128)} async-done(((f32[128,6144]{1,0:T(8,128)}), f32[32,6144]{1,0:T(8,128)}) %reduce-scatter.3.cloned.1.call-update) | async-done | bytes 786448 | tf_op jit(solution)/shard_map/reduce_scatter | solution.py:84
  155.2 1.2 fusion.23
  156.4 1.3 collective-permute-start
  157.7 2.3 collective-permute-done
  160.0 0.8 broadcast_select_fusion
  161.6 1.4 fusion.36
  163.0 0.3 fusion.18
  163.4 38.7 %all-gather.4.cloned.1.call-done = bf16[128,6144]{1,0:T(8,128)(2,1)} async-done(((bf16[32,6144]{1,0:T(8,128)(2,1)}), bf16[128,6144]{1,0:T(8,128)(2,1)}) %all-gather.4.cloned.1.call-update) | async-done | bytes 1572880 | tf_op jit(solution)/shard_map/all_gather | solution.py:80
  202.0 8.2 %fusion.6 = f32[128,1536]{1,0:T(8,128)S(1)} fusion(bf16[128,6144]{1,0:T(8,128)(2,1)} %all-gather.4.cloned.1.call-done, bf16[1,6144,1536]{2,1,0:T(8,128)(2,1)} %param.11), kind=kOutput, calls=%fused_computation.6 | convolution fusion | flops 2415919104 | bytes 21233664 | tf_op jit(solution)/shard_map/dot_general | solution.py:81
  210.2 21.4 %all-reduce.3 = bf16[128,1536]{1,0:T(8,128)(2,1)S(1)} all-reduce(f32[128,1536]{1,0:T(8,128)S(1)} %fusion.6), channel_id=1, replica_groups=mesh['section'=4,'row'=2,'col'=4] {'row'}, use_global_device_ids=true, to_apply=%region_8.9 | all-reduce | flops 196608 | bytes 1179648 | tf_op jit(solution)/shard_map/psum | solution.py:82
  231.9 2.4 multiply_reduce_fusion
  234.3 1.7 fusion.21
  236.0 0.2 copy.68
  236.3 10.8 %fusion.2 = f32[128,6144]{1,0:T(8,128)} fusion(bf16[128,1536]{0,1:T(8,128)(2,1)S(1)} %bitcast.59, bf16[1,1536,6144]{2,1,0:T(8,128)(2,1)} %param.12), kind=kOutput, calls=%fused_computation.2 | convolution fusion | flops 2415919104 | bytes 22413312 | tf_op jit(solution)/shard_map/dot_general | solution.py:85
  247.1 60.5 %reduce-scatter.5.cloned.1.call-done = f32[32,6144]{1,0:T(8,128)} async-done(((f32[128,6144]{1,0:T(8,128)}), f32[32,6144]{1,0:T(8,128)}) %reduce-scatter.5.cloned.1.call-update) | async-done | bytes 786448 | tf_op jit(solution)/shard_map/reduce_scatter | solution.py:84
  307.6 2.0 fusion.24
  (35 shorter events, 2.3 us)
Async XLA Ops:
  7.2 7.4 %copy-start = (s32[48,2,3]{0,1,2:T(2,128)S(1)}, s32[48,2,3]{0,1,2:T(2,128)}, u32[]{:S(2)}) copy-start(s32[48,2,3]{0,1,2:T(2,128)} %param.16) | copy-start | bytes 3460
  7.2 42.2 %all-gather.6.cloned.1.call-start = ((), (), s32[]{:S(2)}) async-start(), calls=%async_computation.5 | async-start | bytes 1966080 | tf_op jit(solution)/shard_map/all_gather | solution.py:80
  7.9 147.3 %reduce-scatter.3.cloned.1.call-start = ((), (), s32[]{:S(2)}) async-start(), calls=%async_computation.2 | async-start | bytes 3932160 | tf_op jit(solution)/shard_map/reduce_scatter | solution.py:84
  79.1 76.1 %copy-start.3 = (bf16[1,32,6144]{2,1,0:T(8,128)(2,1)S(1)}, bf16[1,32,6144]{2,1,0:T(8,128)(2,1)}, u32[]{:S(2)}) copy-start(bf16[1,32,6144]{2,1,0:T(8,128)(2,1)} %param.9) | copy-start | bytes 1179652
  81.5 78.6 %copy-start.4 = (bf16[32,6144]{1,0:T(8,128)(2,1)S(1)}, bf16[32,6144]{1,0:T(8,128)(2,1)}, u32[]{:S(2)}) copy-start(bf16[32,6144]{1,0:T(8,128)(2,1)} %param.10) | copy-start | bytes 1179652
  94.7 107.3 %all-gather.4.cloned.1.call-start = ((), (), s32[]{:S(2)}) async-start(), calls=%async_computation.3 | async-start | bytes 1966080 | tf_op jit(solution)/shard_map/all_gather | solution.py:80
  156.4 4.7 %copy-start.5 = (bf16[32,6144]{1,0:T(8,128)(2,1)}, bf16[32,6144]{1,0:T(8,128)(2,1)S(1)}, u32[]{:S(2)}) copy-start(bf16[32,6144]{1,0:T(8,128)(2,1)S(1)} %fusion.23) | copy-start | bytes 1179652
  156.4 3.6 %collective-permute-start = (bf16[32,6144]{1,0:T(8,128)(2,1)S(1)}, bf16[32,6144]{1,0:T(8,128)(2,1)S(1)}, u32[]{:S(2)}, u32[]{:S(2)}) collective-permute-start(bf16[32,6144]{1,0:T(8,128)(2,1)S(1)} %fusion.23), channel_id=1, source_target_pairs={{8,0},{16,8},{24,16},{9,1},{17,9},{25,17},{10,2},{18,10},{26,18},{... | collective-permute-start | bytes 1179656 | tf_op jit(solution)/shard_map/ppermute | solution.py:13
  160.9 146.7 %reduce-scatter.5.cloned.1.call-start = ((), (), s32[]{:S(2)}) async-start(), calls=%async_computation.4 | async-start | bytes 3932160 | tf_op jit(solution)/shard_map/reduce_scatter | solution.py:84
  231.9 75.6 %copy-start.2 = (bf16[32,6144]{1,0:T(8,128)(2,1)S(1)}, bf16[32,6144]{1,0:T(8,128)(2,1)}, u32[]{:S(2)}) copy-start(bf16[32,6144]{1,0:T(8,128)(2,1)} %broadcast_select_fusion) | copy-start | bytes 1179652
  231.9 77.6 %copy-start.1 = (s32[48,2,3]{0,1,2:T(2,128)S(1)}, s32[48,2,3]{0,1,2:T(2,128)}, u32[]{:S(2)}) copy-start(s32[48,2,3]{0,1,2:T(2,128)} %param.16) | copy-start | bytes 3460
Sparse Core Ops, SparseCore 0:
  9.6 39.7 all-gather.5
  94.8 60.3 reduce-scatter.2
  161.0 40.9 all-gather.3
  247.2 60.3 reduce-scatter.4
where the time goes:
time: 317 us; the launch traced here: 316 us
  waiting for transfers between devices  191 us (60%)
  matrix products  51.1 us (16%)
  blocking collectives  42.7 us (13%)
  between operations  17.9 us (6%)
  local copies, waits for them, and re-layouts  7.55 us (2%)
  other arithmetic  4.11 us (1%)
    reduce_scatter x2, waiting for transfers between devices, section_step(): lax.psum_scatter(jnp.dot(dquery, w_query, preferred_element_type=jnp.floa...  121 us
    all_gather x2, waiting for transfers between devices, section_step(): gathered = lax.all_gather(gradient, 'col', axis=0, tiled=True)  67.4 us
    psum x2, blocking collectives, section_step(): upstream = lax.psum(partial_value, 'row').astype(jnp.bfloat16)  42.7 us
    dot_general x2, matrix products, section_step(): jnp.dot(dquery, w_query, preferred_element_type=jnp.float32)  21.6 us
    dot_general x2, matrix products, section_step(): partial_value = jnp.dot(gathered, w_out, preferred_element_type=jnp.float32)  16.4 us
  transfers between devices with their start and end apart: 5, of which 5 were waited for; matrix products, arithmetic and copies ran while one was open for 4% of the time, Pallas kernels for 0%

commit v1 on v0

--- a/solution.py
+++ b/solution.py
@@ -79,7 +79,7 @@
         value_rows = lax.dynamic_index_in_dim(saved_value[:, 0], slot_index, 0, keepdims=False)
         gathered = lax.all_gather(gradient, "col", axis=0, tiled=True)
         partial_value = jnp.dot(gathered, w_out, preferred_element_type=jnp.float32)
-        upstream = lax.psum(partial_value, "row").astype(jnp.bfloat16)
+        upstream = jnp.sum(lax.all_gather(partial_value, "row"), axis=0).astype(jnp.bfloat16)
         dquery = attend_rows(upstream, query_rows, key_rows, value_rows, allowed)
         mixed_back = lax.psum_scatter(
             jnp.dot(dquery, w_query, preferred_element_type=jnp.float32),

time: 317 us -> 333 us (1.050)
  waiting for transfers between devices: 191 us -> 247 us
  blocking collectives: 42.7 us -> 0 us
    all_gather x0 -> x2, waiting for transfers between devices: none -> 45.3 us  [section_step(): lax.all_gather(partial_value, 'row')]
    psum x2 -> x0, blocking collectives: 42.7 us -> none  [section_step(): upstream = lax.psum(partial_value, 'row').astype(jnp.bfloat16)]
    all_gather x2, waiting for transfers between devices: 67.4 us -> 77.3 us  [section_step(): gathered = lax.all_gather(gradient, 'col', axis=0, tiled=True)]
    dot_general x2, matrix products: 16.4 us -> 20.7 us  [section_step(): partial_value = jnp.dot(gathered, w_out, preferred_element_type=jnp.float32)]
  transfers between devices with their start and end apart: 5 -> 7, of which waited for: 5 -> 7; matrix products, arithmetic and copies ran while one was open for 4% -> 2% of each run, Pallas kernels for 0% -> 0%
where the time goes in v1:
time: 333 us; the launch traced here: 332 us
  waiting for transfers between devices  247 us (74%)
  matrix products  52 us (16%)
  between operations  18.3 us (5%)
  other arithmetic  7.23 us (2%)
  local copies, waits for them, and re-layouts  6.03 us (2%)
    reduce_scatter x2, waiting for transfers between devices, section_step(): lax.psum_scatter(jnp.dot(dquery, w_query, preferred_element_type=jnp.floa...  121 us
    all_gather x2, waiting for transfers between devices, section_step(): gathered = lax.all_gather(gradient, 'col', axis=0, tiled=True)  77.3 us
    all_gather x2, waiting for transfers between devices, section_step(): lax.all_gather(partial_value, 'row')  45.3 us
    dot_general x2, matrix products, section_step(): jnp.dot(dquery, w_query, preferred_element_type=jnp.float32)  21.6 us
    dot_general x2, matrix products, section_step(): partial_value = jnp.dot(gathered, w_out, preferred_element_type=jnp.float32)  20.7 us
  transfers between devices with their start and end apart: 7, of which 7 were waited for; matrix products, arithmetic and copies ran while one was open for 2% of the time, Pallas kernels for 0%

profile of v1, /device:TPU:0, one launch (start us, length us, event | category | flops | bytes accessed | tf_op | source)
XLA Modules:
  0.0 332.0 jit_solution(17520406261880376032)
XLA Ops:
  7.2 0.7 all-gather.10.cloned.1.call-update
  8.0 0.8 fusion.34
  8.7 0.6 constant_dynamic-slice_fusion.3
  13.2 36.1 %all-gather.10.cloned.1.call-done = bf16[1,128,6144]{2,1,0:T(8,128)(2,1)} async-done(((bf16[1,32,6144]{2,1,0:T(8,128)(2,1)}), bf16[1,128,6144]{2,1,0:T(8,128)(2,1)}) %all-gather.10.cloned.1.call-update) | async-done | bytes 1572880 | tf_op jit(solution)/shard_map/all_gather | solution.py:80
  49.4 10.4 %fusion.8 = f32[128,1536]{1,0:T(8,128)} fusion(bf16[1,6144,1536]{2,1,0:T(8,128)(2,1)} %param.11, bf16[1,128,6144]{2,1,0:T(8,128)(2,1)} %all-gather.10.cloned.1.call-done), kind=kOutput, calls=%fused_computation.8 | convolution fusion | flops 2415919104 | bytes 21233664 | tf_op jit(solution)/shard_map/dot_general | solution.py:81
  60.9 1.2 constant_dynamic-slice_fusion
  62.4 1.4 fusion.35
  63.8 0.3 fusion.17
  64.1 21.8 %all-gather.12.cloned.1.call-done = f32[256,1536]{1,0:T(8,128)} async-done(((f32[128,1536]{1,0:T(8,128)}), f32[256,1536]{1,0:T(8,128)}) %all-gather.12.cloned.1.call-update) | async-done | bytes 1572880 | tf_op jit(solution)/shard_map/all_gather | solution.py:82
  85.9 1.6 reduce_sum.55
  87.5 0.9 copy.71
  88.4 2.5 multiply_reduce_fusion.1
  90.9 1.7 fusion.22
  92.6 0.2 copy.77
  92.9 10.8 %fusion.4 = f32[128,6144]{1,0:T(8,128)} fusion(bf16[128,1536]{0,1:T(8,128)(2,1)S(1)} %bitcast.60, bf16[1,1536,6144]{2,1,0:T(8,128)(2,1)} %param.12), kind=kOutput, calls=%fused_computation.4 | convolution fusion | flops 2415919104 | bytes 22413312 | tf_op jit(solution)/shard_map/dot_general | solution.py:85
  103.7 60.5 %reduce-scatter.3.cloned.1.call-done = f32[32,6144]{1,0:T(8,128)} async-done(((f32[128,6144]{1,0:T(8,128)}), f32[32,6144]{1,0:T(8,128)}) %reduce-scatter.3.cloned.1.call-update) | async-done | bytes 786448 | tf_op jit(solution)/shard_map/reduce_scatter | solution.py:84
  164.2 1.2 fusion.23
  165.5 1.3 collective-permute-start
  166.8 2.3 collective-permute-done
  169.1 0.8 broadcast_select_fusion
  170.0 41.1 %all-gather.8.cloned.1.call-done = bf16[128,6144]{1,0:T(8,128)(2,1)} async-done(((bf16[32,6144]{1,0:T(8,128)(2,1)}), bf16[128,6144]{1,0:T(8,128)(2,1)}) %all-gather.8.cloned.1.call-update) | async-done | bytes 1572880 | tf_op jit(solution)/shard_map/all_gather | solution.py:80
  211.1 10.4 %fusion.6 = f32[128,1536]{1,0:T(8,128)} fusion(bf16[128,6144]{1,0:T(8,128)(2,1)} %all-gather.8.cloned.1.call-done, bf16[1,6144,1536]{2,1,0:T(8,128)(2,1)} %param.11), kind=kOutput, calls=%fused_computation.6 | convolution fusion | flops 2415919104 | bytes 21233664 | tf_op jit(solution)/shard_map/dot_general | solution.py:81
  222.4 1.4 fusion.36
  223.8 0.3 fusion.18
  224.1 23.5 %all-gather.14.cloned.1.call-done = f32[256,1536]{1,0:T(8,128)} async-done(((f32[128,1536]{1,0:T(8,128)}), f32[256,1536]{1,0:T(8,128)}) %all-gather.14.cloned.1.call-update) | async-done | bytes 1572880 | tf_op jit(solution)/shard_map/all_gather | solution.py:82
  247.7 1.6 reduce_sum.58
  249.5 1.5 multiply_reduce_fusion
  251.0 0.6 fusion.21
  251.6 0.2 copy.88
  251.8 10.8 %fusion.2 = f32[128,6144]{1,0:T(8,128)} fusion(bf16[128,1536]{0,1:T(8,128)(2,1)S(1)} %bitcast.61, bf16[1,1536,6144]{2,1,0:T(8,128)(2,1)} %param.12), kind=kOutput, calls=%fused_computation.2 | convolution fusion | flops 2415919104 | bytes 22413312 | tf_op jit(solution)/shard_map/dot_general | solution.py:85
  262.6 60.6 %reduce-scatter.5.cloned.1.call-done = f32[32,6144]{1,0:T(8,128)} async-done(((f32[128,6144]{1,0:T(8,128)}), f32[32,6144]{1,0:T(8,128)}) %reduce-scatter.5.cloned.1.call-update) | async-done | bytes 786448 | tf_op jit(solution)/shard_map/reduce_scatter | solution.py:84
  323.2 2.0 fusion.24
  (45 shorter events, 2.8 us)
Async XLA Ops:
  7.2 52.9 %copy-start = (s32[48,2,3]{0,1,2:T(2,128)S(1)}, s32[48,2,3]{0,1,2:T(2,128)}, u32[]{:S(2)}) copy-start(s32[48,2,3]{0,1,2:T(2,128)} %param.16) | copy-start | bytes 3460
  7.2 52.6 %copy-start.4 = (bf16[2,1,128,1536]{3,2,1,0:T(8,128)(2,1)S(1)}, bf16[2,1,128,1536]{3,2,1,0:T(8,128)(2,1)}, u32[]{:S(2)}) copy-start(bf16[2,1,128,1536]{3,2,1,0:T(8,128)(2,1)} %param.14) | copy-start | bytes 2359300
  7.2 53.4 %copy-start.5 = (bf16[2,1,128,1536]{3,2,1,0:T(8,128)(2,1)S(1)}, bf16[2,1,128,1536]{3,2,1,0:T(8,128)(2,1)}, u32[]{:S(2)}) copy-start(bf16[2,1,128,1536]{3,2,1,0:T(8,128)(2,1)} %param.13) | copy-start | bytes 2359300
  7.2 42.2 %all-gather.10.cloned.1.call-start = ((), (), s32[]{:S(2)}) async-start(), calls=%async_computation.5 | async-start | bytes 1966080 | tf_op jit(solution)/shard_map/all_gather | solution.py:80
  7.9 78.0 %all-gather.12.cloned.1.call-start = ((), (), s32[]{:S(2)}) async-start(), calls=%async_computation.6 | async-start | bytes 2359296 | tf_op jit(solution)/shard_map/all_gather | solution.py:82
  59.7 104.5 %reduce-scatter.3.cloned.1.call-start = ((), (), s32[]{:S(2)}) async-start(), calls=%async_computation.2 | async-start | bytes 3932160 | tf_op jit(solution)/shard_map/reduce_scatter | solution.py:84
  88.4 75.8 %copy-start.3 = (bf16[1,32,6144]{2,1,0:T(8,128)(2,1)S(1)}, bf16[1,32,6144]{2,1,0:T(8,128)(2,1)}, u32[]{:S(2)}) copy-start(bf16[1,32,6144]{2,1,0:T(8,128)(2,1)} %param.9) | copy-start | bytes 1179652
  92.6 76.5 %copy-start.6 = (bf16[32,6144]{1,0:T(8,128)(2,1)S(1)}, bf16[32,6144]{1,0:T(8,128)(2,1)}, u32[]{:S(2)}) copy-start(bf16[32,6144]{1,0:T(8,128)(2,1)} %param.10) | copy-start | bytes 1179652
  103.7 107.4 %all-gather.8.cloned.1.call-start = ((), (), s32[]{:S(2)}) async-start(), calls=%async_computation.3 | async-start | bytes 1966080 | tf_op jit(solution)/shard_map/all_gather | solution.py:80
  165.5 83.8 %copy-start.7 = (bf16[32,6144]{1,0:T(8,128)(2,1)}, bf16[32,6144]{1,0:T(8,128)(2,1)S(1)}, u32[]{:S(2)}) copy-start(bf16[32,6144]{1,0:T(8,128)(2,1)S(1)} %fusion.23) | copy-start | bytes 1179652
  165.5 3.6 %collective-permute-start = (bf16[32,6144]{1,0:T(8,128)(2,1)S(1)}, bf16[32,6144]{1,0:T(8,128)(2,1)S(1)}, u32[]{:S(2)}, u32[]{:S(2)}) collective-permute-start(bf16[32,6144]{1,0:T(8,128)(2,1)S(1)} %fusion.23), channel_id=1, source_target_pairs={{8,0},{16,8},{24,16},{9,1},{17,9},{25,17},{10,2},{18,10},{26,18},{... | collective-permute-start | bytes 1179656 | tf_op jit(solution)/shard_map/ppermute | solution.py:13
  169.9 77.7 %all-gather.14.cloned.1.call-start = ((), (), s32[]{:S(2)}) async-start(), calls=%async_computation.7 | async-start | bytes 2359296 | tf_op jit(solution)/shard_map/all_gather | solution.py:82
  221.5 101.7 %reduce-scatter.5.cloned.1.call-start = ((), (), s32[]{:S(2)}) async-start(), calls=%async_computation.4 | async-start | bytes 3932160 | tf_op jit(solution)/shard_map/reduce_scatter | solution.py:84
  249.5 73.7 %copy-start.2 = (bf16[32,6144]{1,0:T(8,128)(2,1)S(1)}, bf16[32,6144]{1,0:T(8,128)(2,1)}, u32[]{:S(2)}) copy-start(bf16[32,6144]{1,0:T(8,128)(2,1)} %broadcast_select_fusion) | copy-start | bytes 1179652
  249.5 75.7 %copy-start.1 = (s32[48,2,3]{0,1,2:T(2,128)S(1)}, s32[48,2,3]{0,1,2:T(2,128)}, u32[]{:S(2)}) copy-start(s32[48,2,3]{0,1,2:T(2,128)} %param.16) | copy-start | bytes 3460
Sparse Core Ops, SparseCore 0:
  9.6 39.7 all-gather.9
  59.9 26.0 all-gather.11
  103.8 60.3 reduce-scatter.2
  170.0 40.9 all-gather.7
  221.6 26.0 all-gather.13
  262.7 60.3 reduce-scatter.4
